TPU v7x, 512 devices: a whole 4x4x16 slice. The times are simulated.
512 devices in a mesh: fsdp: 64 (over z_lo, x, core), tp: 8 (over z_hi, y).
Axes of the slice: x: 4, y: 4, z: 16 (z_hi: 2, z_lo: 8; z = z_hi * 8 + z_lo), core: 2. Of those that a mesh axis runs over, the one named last changes fastest.
Arguments:
- gradient: float32 [16384, 8192], P('fsdp', 'tp'), may hold values from -100 to 100
- sign_bits: int32 [8192, 128], P('tp'), may hold values 0 or 1
- block_column: int32 [64], P('tp'), may hold values from 0 to 3, as said below
Outputs:
- projected: float32 [512, 8192], P('fsdp', 'tp')
Inputs may be any that keep to these rules, and one draw needn't show every extreme that they name: `block_column`: each of the 4 column blocks is chosen by at least two blocks of rows.
All inputs are finite; a program needn't handle non-finite values. No bound on the sum of `sign_bits` on one device may be relied on, other than what follows from the above.
Results may differ from a plain program's by a relative error of at most 0.000082.
Values sent between devices are 32-bit elements; how exact they have to be, the bound alone decides.
A program may use at most 64 MiB of HBM per device.

v0:
```python
import jax
import jax.numpy as jnp
from jax import lax
from jax.sharding import PartitionSpec as P

R = 512


HIGHEST = lax.Precision.HIGHEST


def sketch_panel(gradient, sign_bits, block_column):
    row_count, col_count = gradient.shape
    block_width = sign_bits.shape[1]
    blocks_here = col_count // block_width
    sign_table = (
        (2 * sign_bits - 1).astype(jnp.float32).reshape(blocks_here, block_width, block_width)
    )
    mixture = jnp.einsum(
        "rbk,bkj->rbj",
        gradient.reshape(row_count, blocks_here, block_width),
        sign_table,
        precision=HIGHEST,
    )
    chosen = (
        block_column[:, None] == jnp.arange(R // block_width, dtype=jnp.int32)[None, :]
    ).astype(jnp.float32)
    placed = jnp.einsum("rbj,bc->rcj", mixture, chosen, precision=HIGHEST)
    return placed.reshape(row_count, R)


def gram_of(sketch_part):
    return jnp.dot(
        sketch_part.T, sketch_part, precision=HIGHEST, preferred_element_type=jnp.float32
    )


def shards(gradient, sign_bits, block_column):
    partial_sketch = sketch_panel(gradient, sign_bits, block_column)
    slab_sketch = lax.psum(partial_sketch, "tp")
    gram_sum = lax.psum(gram_of(slab_sketch), "fsdp")
    lower_factor = jnp.linalg.cholesky(gram_sum)
    basis_rows = jax.scipy.linalg.solve_triangular(lower_factor, slab_sketch.T, lower=True).T
    return lax.psum_scatter(
        jnp.dot(basis_rows.T, gradient, precision=HIGHEST, preferred_element_type=jnp.float32),
        "fsdp",
        scatter_dimension=0,
        tiled=True,
    )


def solution(mesh):
    return jax.shard_map(
        shards,
        mesh=mesh,
        in_specs=(P("fsdp", "tp"), P("tp", None), P("tp")),
        out_specs=P("fsdp", "tp"),
        check_vma=False,
    )
```

profile of v0, /device:TPU:1, one launch (start us, length us, event | category | flops | bytes accessed | tf_op | source)
XLA Modules:
  0.0 1578.1 jit_solution(13672106299357237187)
XLA Ops:
  6.5 1.6 copy.9
  8.2 1.0 fusion.45
  9.3 0.4 copy.7
  9.7 0.6 fusion.1
  10.3 0.8 copy.12
  11.2 154.8 %all-reduce.4.cloned.1.call-done = f32[256,512]{1,0:T(8,128)} async-done(((f32[256,512]{1,0:T(8,128)}), f32[256,512]{1,0:T(8,128)}) %all-reduce.4.cloned.1.call-update) | async-done | bytes 524304 | tf_op jit(solution)/shard_map/psum | solution.py:40
  166.0 3.3 fusion.46
  169.3 0.2 reduce-scatter.2.cloned.1.call-start
  169.5 830.7 %all-reduce.6.cloned.1.call-done = f32[512,512]{0,1:T(8,128)} async-done(((f32[512,512]{0,1:T(8,128)}), f32[512,512]{0,1:T(8,128)}) %all-reduce.6.cloned.1.call-update) | async-done | bytes 1048592 | tf_op jit(solution)/shard_map/psum | solution.py:41
  1000.2 1.6 copy.5
  1001.9 0.2 fusion
  1002.1 11.7 cholesky.104
  1013.9 9.8 custom-call.31
  1023.7 0.1 cholesky.224
  1023.8 0.3 constant_dynamic-update-slice_fusion.3
  1024.1 0.3 convolution_subtract_fusion
  1024.5 11.7 cholesky.217
  1036.2 10.0 custom-call.32
  1046.2 0.3 convolution_dynamic-update-slice_fusion
  1046.5 0.4 convolution_subtract_fusion.3
  1046.9 11.7 cholesky.238
  1058.7 0.7 compare_reduce_fusion.1
  1059.4 9.8 custom-call.33
  1069.2 0.2 convolution_dynamic-update-slice_fusion.1
  1069.4 0.4 convolution_subtract_fusion.5
  1069.8 11.7 cholesky.255
  1081.6 0.6 compare_reduce_fusion
  1082.2 0.7 compare_reduce_fusion.2
  1085.4 0.4 select_select_fusion
  1085.8 8.1 while.1
  1085.9 0.6 fusion.58
  1086.5 1.3 bitcast_dynamic-update-slice_fusion.2
  1088.0 0.6 fusion.58
  1088.6 1.3 bitcast_dynamic-update-slice_fusion.2
  1090.0 0.6 fusion.58
  1090.6 1.3 bitcast_dynamic-update-slice_fusion.2
  1092.0 0.6 fusion.58
  1092.6 1.3 bitcast_dynamic-update-slice_fusion.2
  1094.0 39.3 %custom-call.34 = f32[4,128,128]{1,2,0:T(8,128)S(1)} custom-call(f32[4,128,128]{2,1,0:T(8,128)S(1)} %get-tuple-element.12), custom_call_target="InvertDiagBlocksLowerTriangular" | custom-call | tf_op jit(solution)/shard_map/jit(_solve_triangular)/triangular_solve | solution.py:43
  1133.3 0.3 fusion.25
  1133.6 0.4 convolution_subtract_fusion.4
  1134.0 0.3 fusion.32
  1134.4 0.6 convolution_subtract_fusion.2
  1134.9 0.3 fusion.30
  1135.3 0.8 convolution_subtract_fusion.1
  1136.1 0.3 fusion.29
  1136.4 3.2 fusion.3
  1139.7 431.9 %reduce-scatter.2.cloned.1.call-done = f32[8,1024]{1,0:T(8,128)} async-done(((f32[512,1024]{1,0:T(8,128)}), f32[8,1024]{1,0:T(8,128)}) %reduce-scatter.2.cloned.1.call-update) | async-done | bytes 32784 | tf_op jit(solution)/shard_map/reduce_scatter | solution.py:44
  (30 shorter events, 0.6 us)
Async XLA Ops:
  6.5 1.6 copy-start.3
  6.5 159.4 %all-reduce.4.cloned.1.call-start = ((), (), s32[]{:S(2)}) async-start(), calls=%async_computation.1 | async-start | bytes 1048576 | tf_op jit(solution)/shard_map/psum | solution.py:40
  8.2 1.5 copy-start.4
  11.2 989.0 %all-reduce.6.cloned.1.call-start = ((), (), s32[]{:S(2)}) async-start(), calls=%async_computation.2 | async-start | bytes 2097152 | tf_op jit(solution)/shard_map/psum | solution.py:41
  169.3 1402.3 %reduce-scatter.2.cloned.1.call-start = ((), (), s32[]{:S(2)}) async-start(), calls=%async_computation.3 | async-start | bytes 2129920 | tf_op jit(solution)/shard_map/reduce_scatter | solution.py:44
  1000.2 1.7 copy-start.2
  1046.9 86.4 %copy-start = (f32[256,512]{1,0:T(8,128)S(1)}, f32[256,512]{1,0:T(8,128)}, u32[]{:S(2)}) copy-start(f32[256,512]{1,0:T(8,128)} %all-reduce.4.cloned.1.call-done) | copy-start | bytes 1572868
  1085.8 50.6 %copy-start.1 = (f32[256,1024]{1,0:T(8,128)S(1)}, f32[256,1024]{1,0:T(8,128)}, u32[]{:S(2)}) copy-start(f32[256,1024]{1,0:T(8,128)} %param.3) | copy-start | bytes 3145732
Sparse Core Ops, SparseCore 0:
  11.3 154.6 all-reduce.3
  169.4 830.7 all-reduce.5
  1139.8 431.7 reduce-scatter.1
where the time goes:
time: 1590 us; the launch traced here: 1580 us
  waiting for transfers between devices  1420 us (89%)
  other arithmetic  119 us (7%)
  between operations  15.9 us (1%)
    psum x1, waiting for transfers between devices, shards(): gram_sum = lax.psum(gram_of(slab_sketch), 'fsdp')  831 us
    reduce_scatter x1, waiting for transfers between devices, shards(): lax.psum_scatter(jnp.dot(basis_rows.T, gradient, precision=HIGHEST, prefe...  432 us
    psum x1, waiting for transfers between devices, shards(): slab_sketch = lax.psum(partial_sketch, 'tp')  155 us
    another operation x14, other arithmetic, shards(): lower_factor = jnp.linalg.cholesky(gram_sum)  78.7 us
    another operation x3, other arithmetic, shards(): jax.scipy.linalg.solve_triangular(lower_factor, slab_sketch.T, lower=True)  39.7 us
  transfers between devices with their start and end apart: 3, of which 3 were waited for; matrix products, arithmetic and copies ran while one was open for 0% of the time, Pallas kernels for 0%

commit v1 on v0

v1 whole, which is shorter than its diff:
```python
import functools

import jax
import jax.numpy as jnp
from jax import lax
from jax.experimental import pallas as pl
from jax.experimental.pallas import tpu as pltpu
from jax.sharding import PartitionSpec as P

MESH = pl.DeviceIdType.MESH
HIGHEST = lax.Precision.HIGHEST
F32 = jnp.float32
BF16 = jnp.bfloat16

R = 512
BLK = 128
NZ, NX, NK, NY, NH = 8, 4, 2, 4, 2
NJ = NX * NK


def position():
    f = lax.axis_index("fsdp")
    t = lax.axis_index("tp")
    j = lax.rem(f, NJ)
    return f, t, lax.div(f, NJ), j, lax.div(j, NK), lax.rem(j, NK), lax.rem(t, NY), lax.div(t, NY)


def entry_barrier(peers):
    barrier = pltpu.get_barrier_semaphore()
    for peer in peers:
        pl.semaphore_signal(barrier, inc=1, device_id=peer, device_id_type=MESH)
    pl.semaphore_wait(barrier, len(peers))


class Sender:
    def __init__(self, send, recv):
        self.send, self.recv, self.copies = send, recv, []

    def put(self, src, dst, device):
        i = len(self.copies)
        copy = pltpu.make_async_remote_copy(
            src_ref=src,
            dst_ref=dst,
            send_sem=self.send.at[i],
            recv_sem=self.recv.at[i],
            device_id=device,
            device_id_type=MESH,
        )
        copy.start()
        self.copies.append(copy)
        return copy

    def drain(self):
        for copy in self.copies:
            copy.wait_send()


def arrive(copies):
    for copy in copies:
        copy.wait_recv()


def split(v):
    hi = v.astype(BF16)
    return hi, (v - hi.astype(F32)).astype(BF16)


def dot(a, b):
    return jnp.dot(a, b, preferred_element_type=F32)


def gather_kernel(
    bc_ref, g_ref, sb_ref, gram_ref, f_ref,
    om, ghi, glo, part, yrecv, q, zrecv, s, st, gp, gr, gz, gbuf, c, ck, d, dx, e, ez, send, recv,
):
    f, t, z, j, x, k, y, h = position()
    rows, cols = g_ref.shape

    def xk(dd):
        return lax.rem(j + dd, NJ)

    def zl(dd):
        return lax.rem(z + dd, NZ)

    def yl(dd):
        return lax.rem(y + dd, NY)

    def xl(dd):
        return lax.rem(x + dd, NX)

    peers = [(f, h * NY + yl(dd)) for dd in range(1, NY)]
    peers += [(f, (1 - h) * NY + y)]
    peers += [(z * NJ + xk(dd), t) for dd in range(1, NJ)]
    peers += [(zl(dd) * NJ + j, t) for dd in range(1, NZ)]
    entry_barrier(peers)
    net = Sender(send, recv)

    for b in range(cols // BLK):
        sign = (2 * sb_ref[b * BLK:(b + 1) * BLK, :] - 1).astype(F32)
        for cb in range(R // BLK):
            here = jnp.where(bc_ref[b] == cb, 1.0, 0.0).astype(F32)
            om[b * BLK:(b + 1) * BLK, cb * BLK:(cb + 1) * BLK] = (sign * here).astype(BF16)
    g = g_ref[...]
    hi, lo = split(g)
    ghi[...] = hi
    glo[...] = lo
    part[...] = (dot(ghi[...], om[...]) + dot(glo[...], om[...])).reshape(part.shape)

    stage = [net.put(part.at[yl(dd)], yrecv.at[dd - 1], (f, h * NY + yl(dd))) for dd in range(1, NY)]
    arrive(stage)
    q[...] = part[y] + yrecv[0] + yrecv[1] + yrecv[2]
    arrive([net.put(q, zrecv, (f, (1 - h) * NY + y))])
    s[y] = q[...] + zrecv[...]
    arrive([net.put(s.at[y], s.at[y], (f, h * NY + yl(dd))) for dd in range(1, NY)])

    whole = s[...].reshape(rows, R)
    st[...] = whole.T
    left = st[pl.ds(pl.multiple_of(y * 128, 128), 128), :]
    right = s[:, :, pl.ds(pl.multiple_of(h * 256, 256), 256)].reshape(rows, 256)
    gp[...] = jnp.dot(left, right, precision=HIGHEST, preferred_element_type=F32).reshape(gp.shape)
    gram_xk = [net.put(gp.at[xk(dd)], gr.at[dd - 1], (z * NJ + xk(dd), t)) for dd in range(1, NJ)]

    shi, slo = split(st[...])
    for n in range(cols // 256):
        gh, gl = ghi[:, n * 256:(n + 1) * 256], glo[:, n * 256:(n + 1) * 256]
        c[:, :, :, n * 256:(n + 1) * 256] = (dot(shi, gh) + (dot(shi, gl) + dot(slo, gh))).reshape(
            NX, NK, R // NJ, 256
        )
    c_k = net.put(c.at[:, 1 - k], ck, (z * NJ + x * NK + 1 - k, t))

    arrive(gram_xk)
    total = gp[j]
    for dd in range(1, NJ):
        total = total + gr[dd - 1]
    gz[z] = total
    gram_z = [net.put(gz.at[z], gz.at[z], (zl(dd) * NJ + j, t)) for dd in range(1, NZ)]

    arrive([c_k])
    d[...] = c[:, k] + ck[...]

    arrive(gram_z)
    total = gz[0]
    for i in range(1, NZ):
        total = total + gz[i]
    gbuf[h, y, x, k] = total
    arrive([net.put(gbuf.at[h, y, x, k], gbuf.at[h, y, x, k], (f, (1 - h) * NY + y))])
    arrive(
        [net.put(gbuf.at[:, y, x, k], gbuf.at[:, y, x, k], (f, h * NY + yl(dd))) for dd in range(1, NY)]
    )
    arrive(
        [
            net.put(gbuf.at[:, :, x, k], gbuf.at[:, :, x, k], (z * NJ + xl(dd) * NK + k, t))
            for dd in range(1, NX)
        ]
    )
    gram_k = net.put(gbuf.at[:, :, :, k], gbuf.at[:, :, :, k], (z * NJ + x * NK + 1 - k, t))

    c_x = [net.put(d.at[xl(dd)], dx.at[dd - 1], (z * NJ + xl(dd) * NK + k, t)) for dd in range(1, NX)]
    arrive([gram_k])
    gram_ref[...] = gbuf[...]
    arrive(c_x)
    slab = d[x] + dx[0] + dx[1] + dx[2]
    for n in range(NZ):
        e[n] = slab[:, n * BLK:(n + 1) * BLK]
    arrive([net.put(e.at[zl(dd)], ez.at[dd - 1], (zl(dd) * NJ + j, t)) for dd in range(1, NZ)])
    total = e[z]
    for dd in range(1, NZ):
        total = total + ez[dd - 1]
    f_ref[...] = total
    net.drain()


def scatter_kernel(y_ref, o_ref, yr, hz, ob, send, recv):
    f, t, z, j, x, k, y, h = position()

    def xk(dd):
        return lax.rem(j + dd, NJ)

    def zl(dd):
        return lax.rem(z + dd, NZ)

    entry_barrier(
        [(z * NJ + xk(dd), t) for dd in range(1, NJ)] + [(zl(dd) * NJ + j, t) for dd in range(1, NZ)]
    )
    net = Sender(send, recv)
    arrive([net.put(y_ref.at[:, xk(dd)], yr.at[dd - 1], (z * NJ + xk(dd), t)) for dd in range(1, NJ)])
    total = y_ref[:, j]
    for dd in range(1, NJ):
        total = total + yr[dd - 1]
    hz[...] = total
    ob[z] = hz[z]
    arrive([net.put(hz.at[zl(dd)], ob.at[z], (zl(dd) * NJ + j, t)) for dd in range(1, NZ)])
    for n in range(NZ):
        o_ref[:, n * BLK:(n + 1) * BLK] = ob[n]
    net.drain()


def shards(gradient, sign_bits, block_column):
    rows, cols = gradient.shape
    vmem = pl.BlockSpec(memory_space=pltpu.VMEM)
    n_sems = 64
    gram_shape = (NH, NY, NX, NK, 16, 256)
    gram, slab = pl.pallas_call(
        gather_kernel,
        out_shape=(
            jax.ShapeDtypeStruct(gram_shape, F32),
            jax.ShapeDtypeStruct((R // NJ, BLK), F32),
        ),
        in_specs=[pl.BlockSpec(memory_space=pltpu.SMEM), vmem, vmem],
        out_specs=(vmem, vmem),
        scratch_shapes=[
            pltpu.VMEM((cols, R), BF16),
            pltpu.VMEM((rows, cols), BF16),
            pltpu.VMEM((rows, cols), BF16),
            pltpu.VMEM((NY, rows // NY, R), F32),
            pltpu.VMEM((NY - 1, rows // NY, R), F32),
            pltpu.VMEM((rows // NY, R), F32),
            pltpu.VMEM((rows // NY, R), F32),
            pltpu.VMEM((NY, rows // NY, R), F32),
            pltpu.VMEM((R, rows), F32),
            pltpu.VMEM((NJ, 16, 256), F32),
            pltpu.VMEM((NJ - 1, 16, 256), F32),
            pltpu.VMEM((NZ, 16, 256), F32),
            pltpu.VMEM(gram_shape, F32),
            pltpu.VMEM((NX, NK, R // NJ, cols), F32),
            pltpu.VMEM((NX, R // NJ, cols), F32),
            pltpu.VMEM((NX, R // NJ, cols), F32),
            pltpu.VMEM((NX - 1, R // NJ, cols), F32),
            pltpu.VMEM((NZ, R // NJ, BLK), F32),
            pltpu.VMEM((NZ - 1, R // NJ, BLK), F32),
            pltpu.SemaphoreType.DMA((n_sems,)),
            pltpu.SemaphoreType.DMA((n_sems,)),
        ],
        compiler_params=pltpu.CompilerParams(
            collective_id=0, has_side_effects=True, vmem_limit_bytes=48 * 1024 * 1024
        ),
        name="gather",
    )(block_column, gradient, sign_bits)
    halves = gram.reshape(NH, R, 256)
    whole = jnp.concatenate([halves[0], halves[1]], axis=1)
    lower = jnp.linalg.cholesky(whole)
    j = lax.rem(lax.axis_index("fsdp"), NJ)
    rhs = lax.dynamic_update_slice(jnp.zeros((R, BLK), F32), slab, (j * (R // NJ), 0))
    solved = jax.scipy.linalg.solve_triangular(lower, rhs, lower=True)
    return pl.pallas_call(
        scatter_kernel,
        out_shape=jax.ShapeDtypeStruct((R // (NZ * NJ), cols), F32),
        in_specs=[vmem],
        out_specs=vmem,
        scratch_shapes=[
            pltpu.VMEM((NJ - 1, NZ, 8, BLK), F32),
            pltpu.VMEM((NZ, 8, BLK), F32),
            pltpu.VMEM((NZ, 8, BLK), F32),
            pltpu.SemaphoreType.DMA((NJ + NZ,)),
            pltpu.SemaphoreType.DMA((NJ + NZ,)),
        ],
        compiler_params=pltpu.CompilerParams(collective_id=1, has_side_effects=True),
        name="scatter",
    )(solved.reshape(NZ, NJ, 8, BLK))


def solution(mesh):
    return jax.shard_map(
        shards,
        mesh=mesh,
        in_specs=(P("fsdp", "tp"), P("tp", None), P("tp")),
        out_specs=P("fsdp", "tp"),
        check_vma=False,
    )
```

time: 1590 us -> 259 us (0.16)
  waiting for transfers between devices: 1420 us -> 0 us
  Pallas kernels: 0 us -> 119 us
    psum x2 -> x0, waiting for transfers between devices: 985 us -> none  [the longest x1 831 us: shards(): gram_sum = lax.psum(gram_of(slab_sketch), 'fsdp')]
    reduce_scatter x1 -> x0, waiting for transfers between devices: 432 us -> none  [shards(): lax.psum_scatter(jnp.dot(basis_rows.T, gradient, precision=HIGHEST, prefe...]
    pallas_call x0 -> x2, Pallas kernels: none -> 119 us  [the longest x1 96.1 us: shards(): pl.pallas_call(gather_kernel, out_shape=(jax.ShapeDtypeStruct(gram_shape,...]
    another operation x17 -> x18, other arithmetic: 118 us -> 119 us  [the longest x14 78.8 us: shards(): lower = jnp.linalg.cholesky(whole)]
  transfers between devices with their start and end apart: 3 -> 0, of which waited for: 3 -> 0; matrix products, arithmetic and copies ran while one was open for 0% -> 0% of each run, Pallas kernels for 0% -> 0%
where the time goes in v1:
time: 259 us
  Pallas kernels  119 us (46%)
  other arithmetic  119 us (46%)
  local copies, waits for them, and re-layouts  13.3 us (5%)
  matrix products  3.8 us (1%)
  between operations  2.94 us (1%)
    pallas_call x1, Pallas kernels, shards(): pl.pallas_call(gather_kernel, out_shape=(jax.ShapeDtypeStruct(gram_shape,...  96.1 us
    another operation x14, other arithmetic, shards(): lower = jnp.linalg.cholesky(whole)  78.8 us
    another operation x4, other arithmetic, shards(): solved = jax.scipy.linalg.solve_triangular(lower, rhs, lower=True)  40.2 us
    pallas_call x1, Pallas kernels, shards(): pl.pallas_call(scatter_kernel, out_shape=jax.ShapeDtypeStruct((R // (NZ *...  23.1 us
    another operation x12, local copies, waits for them, and re-layouts  8.06 us

profile of v1, /device:TPU:1, one launch (start us, length us, event | category | flops | bytes accessed | tf_op | source)
XLA Modules:
  0.0 258.6 jit_solution(5136727747632395247)
XLA Ops:
  0.0 1.2 copy-done
  1.2 1.0 copy-done.1
  2.3 0.7 copy-done.2
  2.9 96.1 %gather.4 = (f32[2,4,4,2,16,256]{5,4,3,2,1,0:T(8,128)S(1)}, f32[64,128]{1,0:T(8,128)S(1)}) custom-call(s32[8]{0:T(128)S(1)} %copy-done.2, f32[256,1024]{1,0:T(8,128)S(1)} %copy-done, s32[1024,128]{1,0:T(8,128)S(1)} %copy-done.1), custom_call_target="tpu_custom_call" | custom-call | tf_op jit(solution)/shard_map/gather/pallas_call | solution.py:203
  99.1 0.1 fusion.31
  99.2 0.2 copy.7
  99.4 0.2 copy.8
  99.6 0.3 copy.9
  100.0 0.2 fusion
  100.2 11.7 %cholesky.104 = f32[128,128]{1,0:T(8,128)S(1)} custom-call(f32[128,128]{1,0:T(8,128)S(1)} %cholesky.266), custom_call_target="Cholesky" | custom-call | tf_op jit(solution)/shard_map/jit(cholesky)/cholesky | solution.py:241
  112.0 9.8 %custom-call.31 = f32[1,128,128]{1,2,0:T(8,128)S(1)} custom-call(f32[1,128,128]{2,1,0:T(8,128)S(1)} %get-tuple-element.38), custom_call_target="InvertDiagBlocksLowerTriangular" | custom-call | tf_op jit(solution)/shard_map/jit(cholesky)/cholesky | solution.py:241
  121.8 0.1 cholesky.224
  121.9 0.3 constant_dynamic-update-slice_fusion.3
  122.2 0.3 convolution_subtract_fusion
  122.6 11.9 %cholesky.217 = f32[128,128]{1,0:T(8,128)S(1)} custom-call(f32[128,128]{1,0:T(8,128)S(1)} %cholesky.270), custom_call_target="Cholesky" | custom-call | tf_op jit(solution)/shard_map/jit(cholesky)/cholesky | solution.py:241
  134.5 0.7 compare_reduce_fusion.2
  136.6 9.8 %custom-call.32 = f32[1,128,128]{1,2,0:T(8,128)S(1)} custom-call(f32[1,128,128]{2,1,0:T(8,128)S(1)} %get-tuple-element.35), custom_call_target="InvertDiagBlocksLowerTriangular" | custom-call | tf_op jit(solution)/shard_map/jit(cholesky)/cholesky | solution.py:241
  146.4 0.3 convolution_dynamic-update-slice_fusion
  146.6 0.4 convolution_subtract_fusion.1
  147.0 11.7 %cholesky.238 = f32[128,128]{1,0:T(8,128)S(1)} custom-call(f32[128,128]{1,0:T(8,128)S(1)} %cholesky.275), custom_call_target="Cholesky" | custom-call | tf_op jit(solution)/shard_map/jit(cholesky)/cholesky | solution.py:241
  158.8 0.6 compare_reduce_fusion.1
  160.1 9.8 %custom-call.33 = f32[1,128,128]{1,2,0:T(8,128)S(1)} custom-call(f32[1,128,128]{2,1,0:T(8,128)S(1)} %get-tuple-element.32), custom_call_target="InvertDiagBlocksLowerTriangular" | custom-call | tf_op jit(solution)/shard_map/jit(cholesky)/cholesky | solution.py:241
  169.9 0.2 convolution_dynamic-update-slice_fusion.1
  170.1 0.4 convolution_subtract_fusion.5
  170.5 11.9 %cholesky.255 = f32[128,128]{1,0:T(8,128)S(1)} custom-call(f32[128,128]{1,0:T(8,128)S(1)} %convolution_subtract_fusion.5), custom_call_target="Cholesky" | custom-call | tf_op jit(solution)/shard_map/jit(cholesky)/cholesky | solution.py:241
  182.5 0.6 compare_reduce_fusion
  183.7 0.1 select_select_fusion
  183.9 8.1 %while.1 = (s32[]{:T(128)}, f32[512,512]{1,0:T(8,128)S(1)}, s32[4,2]{0,1:T(2,128)S(1)}, f32[4,128,128]{2,1,0:T(8,128)S(1)}, s32[]{:T(128)}) while((s32[]{:T(128)}, f32[512,512]{1,0:T(8,128)S(1)}, s32[4,2]{0,1:T(2,128)S(1)}, f32[4,128,128]{2,1,0:T(8,128)S(1)}, s32[]{:T(128)}) %tuple.28), condition=%wide.while_cond, body=%wide.while_body.sunk | while | flops 2 | bytes 131181 | solution.py:244
  183.9 0.1 constant_dynamic-slice_fusion.2
  184.0 0.6 fusion.38
  184.6 1.3 bitcast_dynamic-update-slice_fusion.2
  186.0 0.6 fusion.38
  186.6 1.3 bitcast_dynamic-update-slice_fusion.2
  188.1 0.6 fusion.38
  188.7 1.3 bitcast_dynamic-update-slice_fusion.2
  190.1 0.6 fusion.38
  190.7 1.3 bitcast_dynamic-update-slice_fusion.2
  192.1 39.3 %custom-call.34 = f32[4,128,128]{1,2,0:T(8,128)S(1)} custom-call(f32[4,128,128]{2,1,0:T(8,128)S(1)} %get-tuple-element.16), custom_call_target="InvertDiagBlocksLowerTriangular" | custom-call | tf_op jit(solution)/shard_map/jit(_solve_triangular)/triangular_solve | solution.py:244
  231.4 0.3 fusion.21
  231.7 0.2 convolution_subtract_fusion.3
  232.0 0.3 fusion.20
  232.2 0.3 convolution_subtract_fusion.2
  232.5 0.3 fusion.18
  232.8 0.3 convolution_subtract_fusion.4
  233.1 0.3 fusion.17
  233.4 0.7 pad_maximum_fusion.1
  234.1 23.1 %scatter.1 = f32[8,1024]{1,0:T(8,128)} custom-call(f32[8,8,8,128]{3,2,1,0:T(8,128)} %bitcast.53), custom_call_target="tpu_custom_call" | custom-call | tf_op jit(solution)/shard_map/scatter/pallas_call | solution.py:245
  257.2 1.4 copy.25
  (19 shorter events, 0.5 us)
Async XLA Ops:
  0.0 1.2 copy-start
  1.2 1.0 copy-start.1
  2.3 0.7 copy-start.2

commit v2 on v1

--- a/solution.py
+++ b/solution.py
@@ -69,9 +69,71 @@
     return jnp.dot(a, b, preferred_element_type=F32)
 
 
-def gather_kernel(
-    bc_ref, g_ref, sb_ref, gram_ref, f_ref,
-    om, ghi, glo, part, yrecv, q, zrecv, s, st, gp, gr, gz, gbuf, c, ck, d, dx, e, ez, send, recv,
+def factor_block(a, ub, p):
+    base = BLK * p
+    tiles = (R + BLK - base) // BLK
+    sub = lax.broadcasted_iota(jnp.int32, (8, BLK), 0)
+    lane = lax.broadcasted_iota(jnp.int32, (8, BLK), 1)
+
+    def spread(v):
+        return jnp.broadcast_to(v, (8, BLK))
+
+    def columns(tile):
+        return slice(base + BLK * tile, base + BLK * (tile + 1))
+
+    def panel(q, rows):
+        here = pl.multiple_of(base + 8 * q, 8)
+        following = pl.multiple_of(base + 8 * jnp.minimum(q + 1, BLK // 8 - 1), 8)
+        rows = list(rows)
+        keep = (lane >= 8 * (q + 1)) & (q > 0)
+        coef = jnp.where(keep, -ub[:, columns(0)], 0.0).T
+        for g in range(1, BLK // 8):
+            ms = [spread(coef[8 * g:8 * g + 8, i:i + 1]) for i in range(8)]
+            at = slice(base + 8 * g, base + 8 * g + 8)
+            for tile in range(tiles):
+                acc = a[at, columns(tile)]
+                for i in range(8):
+                    acc = acc + ms[i] * spread(ub[i:i + 1, columns(tile)])
+                a[at, columns(tile)] = acc
+        head = pltpu.roll(rows[0], BLK - 8 * q, 1)
+        flip = head.T
+        c = [spread(head[:, i:i + 1]) for i in range(8)]
+        x = [spread(flip[8:16, i:i + 1]) for i in range(8)]
+        ahead = [jnp.zeros((8, BLK), F32) for _ in range(tiles)]
+        for i in range(8):
+            rs = lax.rsqrt(spread(c[i][i:i + 1, :]))
+            li, yi = c[i] * rs, x[i] * rs
+            for kk in range(i + 1, 8):
+                lk = spread(c[i][kk:kk + 1, :]) * rs
+                c[kk] = c[kk] - li * lk
+                x[kk] = x[kk] - yi * lk
+            low = jnp.where(sub > i, li, 0.0)
+            for tile in range(tiles):
+                row = spread(rows[tile][i:i + 1, :]) * rs
+                rows[tile] = jnp.where(sub == i, row, rows[tile] - low * row)
+                ahead[tile] = ahead[tile] + yi * row
+        out = []
+        for tile in range(tiles):
+            a[pl.ds(here, 8), columns(tile)] = rows[tile]
+            ub[:, columns(tile)] = rows[tile]
+            out.append(a[pl.ds(following, 8), columns(tile)] - ahead[tile])
+        return tuple(out)
+
+    first = tuple(a[base:base + 8, columns(tile)] for tile in range(tiles))
+    lax.fori_loop(0, BLK // 8, panel, first)
+    if base + BLK < R:
+        below = slice(base + BLK, R)
+        right = slice(base + BLK, R + BLK)
+        done = slice(base, base + BLK)
+        a[below, right] = a[below, right] - jnp.dot(
+            a[done, below].T, a[done, right], precision=HIGHEST, preferred_element_type=F32
+        )
+
+
+def refresh_kernel(
+    bc_ref, g_ref, sb_ref, o_ref,
+    om, ghi, glo, part, yrecv, q, zrecv, s, st, gp, gr, gz, gbuf, c, ck, d, dx, e, ez,
+    a, ub, yb, yr, hz, ob, send, recv,
 ):
     f, t, z, j, x, k, y, h = position()
     rows, cols = g_ref.shape
@@ -157,34 +219,32 @@
 
     c_x = [net.put(d.at[xl(dd)], dx.at[dd - 1], (z * NJ + xl(dd) * NK + k, t)) for dd in range(1, NX)]
     arrive([gram_k])
-    gram_ref[...] = gbuf[...]
+
+    for half in range(NH):
+        a[:, half * 256:(half + 1) * 256] = gbuf[half].reshape(R, 256)
+    chunk = R // NJ
+    down = lax.broadcasted_iota(jnp.int32, (R, BLK), 0) - chunk * j
+    across = lax.broadcasted_iota(jnp.int32, (R, BLK), 1)
+    a[:, R:] = jnp.where((down == across) & (across < chunk), 1.0, 0.0)
+    ub[...] = jnp.zeros_like(ub)
+    factor_block(a, ub, 0)
     arrive(c_x)
     slab = d[x] + dx[0] + dx[1] + dx[2]
     for n in range(NZ):
         e[n] = slab[:, n * BLK:(n + 1) * BLK]
-    arrive([net.put(e.at[zl(dd)], ez.at[dd - 1], (zl(dd) * NJ + j, t)) for dd in range(1, NZ)])
+    c_z = [net.put(e.at[zl(dd)], ez.at[dd - 1], (zl(dd) * NJ + j, t)) for dd in range(1, NZ)]
+    for p in range(1, R // BLK):
+        factor_block(a, ub, p)
+    arrive(c_z)
     total = e[z]
     for dd in range(1, NZ):
         total = total + ez[dd - 1]
-    f_ref[...] = total
-    net.drain()
-
-
-def scatter_kernel(y_ref, o_ref, yr, hz, ob, send, recv):
-    f, t, z, j, x, k, y, h = position()
-
-    def xk(dd):
-        return lax.rem(j + dd, NJ)
-
-    def zl(dd):
-        return lax.rem(z + dd, NZ)
-
-    entry_barrier(
-        [(z * NJ + xk(dd), t) for dd in range(1, NJ)] + [(zl(dd) * NJ + j, t) for dd in range(1, NZ)]
-    )
-    net = Sender(send, recv)
-    arrive([net.put(y_ref.at[:, xk(dd)], yr.at[dd - 1], (z * NJ + xk(dd), t)) for dd in range(1, NJ)])
-    total = y_ref[:, j]
+    yb[...] = jnp.dot(
+        a[:, R:R + chunk], total, precision=HIGHEST, preferred_element_type=F32
+    ).reshape(yb.shape)
+
+    arrive([net.put(yb.at[:, xk(dd)], yr.at[dd - 1], (z * NJ + xk(dd), t)) for dd in range(1, NJ)])
+    total = yb[:, j]
     for dd in range(1, NJ):
         total = total + yr[dd - 1]
     hz[...] = total
@@ -198,16 +258,13 @@
 def shards(gradient, sign_bits, block_column):
     rows, cols = gradient.shape
     vmem = pl.BlockSpec(memory_space=pltpu.VMEM)
-    n_sems = 64
+    n_sems = 80
     gram_shape = (NH, NY, NX, NK, 16, 256)
-    gram, slab = pl.pallas_call(
-        gather_kernel,
-        out_shape=(
-            jax.ShapeDtypeStruct(gram_shape, F32),
-            jax.ShapeDtypeStruct((R // NJ, BLK), F32),
-        ),
+    return pl.pallas_call(
+        refresh_kernel,
+        out_shape=jax.ShapeDtypeStruct((R // (NZ * NJ), cols), F32),
         in_specs=[pl.BlockSpec(memory_space=pltpu.SMEM), vmem, vmem],
-        out_specs=(vmem, vmem),
+        out_specs=vmem,
         scratch_shapes=[
             pltpu.VMEM((cols, R), BF16),
             pltpu.VMEM((rows, cols), BF16),
@@ -228,35 +285,20 @@
             pltpu.VMEM((NX - 1, R // NJ, cols), F32),
             pltpu.VMEM((NZ, R // NJ, BLK), F32),
             pltpu.VMEM((NZ - 1, R // NJ, BLK), F32),
+            pltpu.VMEM((R, R + BLK), F32),
+            pltpu.VMEM((8, R + BLK), F32),
+            pltpu.VMEM((NZ, NJ, 8, BLK), F32),
+            pltpu.VMEM((NJ - 1, NZ, 8, BLK), F32),
+            pltpu.VMEM((NZ, 8, BLK), F32),
+            pltpu.VMEM((NZ, 8, BLK), F32),
             pltpu.SemaphoreType.DMA((n_sems,)),
             pltpu.SemaphoreType.DMA((n_sems,)),
         ],
         compiler_params=pltpu.CompilerParams(
             collective_id=0, has_side_effects=True, vmem_limit_bytes=48 * 1024 * 1024
         ),
-        name="gather",
+        name="refresh",
     )(block_column, gradient, sign_bits)
-    halves = gram.reshape(NH, R, 256)
-    whole = jnp.concatenate([halves[0], halves[1]], axis=1)
-    lower = jnp.linalg.cholesky(whole)
-    j = lax.rem(lax.axis_index("fsdp"), NJ)
-    rhs = lax.dynamic_update_slice(jnp.zeros((R, BLK), F32), slab, (j * (R // NJ), 0))
-    solved = jax.scipy.linalg.solve_triangular(lower, rhs, lower=True)
-    return pl.pallas_call(
-        scatter_kernel,
-        out_shape=jax.ShapeDtypeStruct((R // (NZ * NJ), cols), F32),
-        in_specs=[vmem],
-        out_specs=vmem,
-        scratch_shapes=[
-            pltpu.VMEM((NJ - 1, NZ, 8, BLK), F32),
-            pltpu.VMEM((NZ, 8, BLK), F32),
-            pltpu.VMEM((NZ, 8, BLK), F32),
-            pltpu.SemaphoreType.DMA((NJ + NZ,)),
-            pltpu.SemaphoreType.DMA((NJ + NZ,)),
-        ],
-        compiler_params=pltpu.CompilerParams(collective_id=1, has_side_effects=True),
-        name="scatter",
-    )(solved.reshape(NZ, NJ, 8, BLK))
 
 
 def solution(mesh):

time: 259 us -> 135 us (0.52)
  other arithmetic: 119 us -> 0 us
  Pallas kernels: 119 us -> 131 us
  local copies, waits for them, and re-layouts: 13.3 us -> 3.54 us
  matrix products: 3.8 us -> 0 us
  between operations: 2.94 us -> 0.01 us
    another operation x18 -> x0, other arithmetic: 119 us -> none  [the longest x14 78.8 us: shards(): lower = jnp.linalg.cholesky(whole)]
    pallas_call x2 -> x1, Pallas kernels: 119 us -> 131 us  [shards(): pl.pallas_call(refresh_kernel, out_shape=jax.ShapeDtypeStruct((R // (NZ *...]
    another operation x17 -> x0, local copies, waits for them, and re-layouts: 8.2 us -> none
    another operation x13 -> x0, matrix products: 3.8 us -> none  [the longest x7 1.93 us: shards(): solved = jax.scipy.linalg.solve_triangular(lower, rhs, lower=True)]
where the time goes in v2:
time: 135 us
  Pallas kernels  131 us (97%)
  local copies, waits for them, and re-layouts  3.54 us (3%)
    pallas_call x1, Pallas kernels, shards(): pl.pallas_call(refresh_kernel, out_shape=jax.ShapeDtypeStruct((R // (NZ *...  131 us
    unnamed x7, local copies, waits for them, and re-layouts  3.54 us

profile of v2, /device:TPU:1, one launch (start us, length us, event | category | flops | bytes accessed | tf_op | source)
XLA Modules:
  0.0 134.8 jit_solution(9022650454670269609)
XLA Ops:
  0.0 0.0 copy-start
  0.0 1.2 copy-done
  1.2 0.0 copy-start.1
  1.2 1.0 copy-done.1
  2.3 0.0 copy-start.2
  2.3 0.7 copy-done.2
  2.9 131.2 %refresh.1 = f32[8,1024]{1,0:T(8,128)S(1)} custom-call(s32[8]{0:T(128)S(1)} %copy-done.2, f32[256,1024]{1,0:T(8,128)S(1)} %copy-done, s32[1024,128]{1,0:T(8,128)S(1)} %copy-done.1), custom_call_target="tpu_custom_call" | custom-call | tf_op jit(solution)/shard_map/refresh/pallas_call | solution.py:263
  134.1 0.6 copy.5
Async XLA Ops:
  0.0 1.2 copy-start
  1.2 1.0 copy-start.1
  2.3 0.7 copy-start.2

commit v3 on v2

v3 whole, which is shorter than its diff:
```python
import functools

import jax
import jax.numpy as jnp
from jax import lax
from jax.experimental import pallas as pl
from jax.experimental.pallas import tpu as pltpu
from jax.sharding import PartitionSpec as P

MESH = pl.DeviceIdType.MESH
HIGHEST = lax.Precision.HIGHEST
F32 = jnp.float32
BF16 = jnp.bfloat16

R = 512
BLK = 128
SUB = 64
NZ, NX, NK, NY, NH = 8, 4, 2, 4, 2
NJ = NX * NK
NM = NY * NJ
NT = NH * NZ


def position():
    f = lax.axis_index("fsdp")
    t = lax.axis_index("tp")
    j = lax.rem(f, NJ)
    return f, t, lax.div(f, NJ), j, lax.div(j, NK), lax.rem(j, NK), lax.rem(t, NY), lax.div(t, NY)


class Sender:
    def __init__(self, send, recv):
        self.send, self.recv, self.copies = send, recv, []

    def put(self, src, dst, device):
        i = len(self.copies)
        copy = pltpu.make_async_remote_copy(
            src_ref=src,
            dst_ref=dst,
            send_sem=self.send.at[i],
            recv_sem=self.recv.at[i],
            device_id=device,
            device_id_type=MESH,
        )
        copy.start()
        self.copies.append(copy)
        return copy

    def drain(self):
        for copy in self.copies:
            copy.wait_send()


def arrive(copies):
    for copy in copies:
        copy.wait_recv()


def split(v):
    hi = v.astype(BF16)
    return hi, (v - hi.astype(F32)).astype(BF16)


def dot(a, b):
    return jnp.dot(a, b, preferred_element_type=F32)


def strip(a, base, at):
    sub = lax.broadcasted_iota(jnp.int32, (8, BLK), 0)
    groups, tiles, lead = SUB // 8, (R + BLK - base) // BLK, at - base

    def spread(v):
        return jnp.broadcast_to(v, (8, BLK))

    def place(g, tile):
        return slice(at + 8 * g, at + 8 * g + 8), slice(base + BLK * tile, base + BLK * (tile + 1))

    rows = [[a[place(g, tile)] for tile in range(tiles)] for g in range(groups)]
    for g in range(groups):
        later = range(groups - g)
        lane = lead + 8 * g
        col = [[spread(rows[g + w][0][:, lane + i:lane + i + 1]) for i in range(8)] for w in later]
        for i in range(8):
            rs = lax.rsqrt(spread(col[0][i][i:i + 1, :]))
            l = [col[w][i] * rs for w in later]
            for n in range(i + 1, 8):
                ln = spread(col[0][i][n:n + 1, :]) * rs
                for w in later:
                    col[w][n] = col[w][n] - l[w] * ln
            low = jnp.where(sub > i, l[0], 0.0)
            for tile in range(tiles):
                row = spread(rows[g][tile][i:i + 1, :]) * rs
                rows[g][tile] = jnp.where(sub == i, row, rows[g][tile] - low * row)
                for w in later[1:]:
                    rows[g + w][tile] = rows[g + w][tile] - l[w] * row
    for g in range(groups):
        for tile in range(tiles):
            a[place(g, tile)] = rows[g][tile]


def take_off(a, done, rest, right):
    a[rest, right] = a[rest, right] - jnp.dot(
        a[done, rest].T, a[done, right], precision=HIGHEST, preferred_element_type=F32
    )


def factor(a):
    end = R + BLK
    for base in range(0, R, BLK):
        for at in range(base, base + BLK, SUB):
            strip(a, base, at)
            if at + SUB < base + BLK:
                take_off(a, slice(at, at + SUB), slice(at + SUB, base + BLK), slice(base, end))
        if base + BLK < R:
            take_off(a, slice(base, base + BLK), slice(base + BLK, R), slice(base + BLK, end))


def refresh_kernel(
    bc_ref, g_hbm, sb_hbm, o_ref,
    g_ref, sb_ref, om, ghi, glo, part, yrecv, q, zrecv, s, st, gp, gr, gz, gbuf, c, ck, d, dx, e, ez,
    a, yb, yr, hz, ob, send, recv, local,
):
    f, t, z, j, x, k, y, h = position()
    rows, cols = g_ref.shape
    m, zz = y * NJ + j, h * NZ + z

    def at_z(dd):
        w = lax.rem(zz + dd, NT)
        return lax.rem(w, NZ) * NJ + j, lax.div(w, NZ) * NY + y

    def zl(dd):
        return lax.rem(z + dd, NZ)

    def at_zl(dd):
        return zl(dd) * NJ + j, t

    def ml(dd):
        return lax.rem(m + dd, NM)

    def at_m(dd):
        w = ml(dd)
        return z * NJ + lax.rem(w, NJ), h * NY + lax.div(w, NJ)

    def jl(dd):
        return lax.rem(j + dd, NJ)

    def at_j(dd):
        return z * NJ + jl(dd), t

    def yl(dd):
        return lax.rem(y + dd, NY)

    def at_y(dd):
        return f, h * NY + yl(dd)

    def xl(dd):
        return lax.rem(x + dd, NX)

    def at_yx(dy, dx):
        return z * NJ + xl(dx) * NK + k, h * NY + yl(dy)

    partner = (z * NJ + x * NK + 1 - k, t)
    loads = [
        pltpu.make_async_copy(g_hbm, g_ref, local.at[0]),
        pltpu.make_async_copy(sb_hbm, sb_ref, local.at[1]),
    ]
    for load in loads:
        load.start()
    peers = [at_m(dd) for dd in range(1, NM)] + [at_z(dd) for dd in range(1, NT)]
    barrier = pltpu.get_barrier_semaphore()
    for peer in peers:
        pl.semaphore_signal(barrier, inc=1, device_id=peer, device_id_type=MESH)

    for load in loads:
        load.wait()
    for b in range(cols // BLK):
        sign = (2 * sb_ref[b * BLK:(b + 1) * BLK, :] - 1).astype(F32)
        for cb in range(R // BLK):
            here = jnp.where(bc_ref[b] == cb, 1.0, 0.0).astype(F32)
            om[b * BLK:(b + 1) * BLK, cb * BLK:(cb + 1) * BLK] = (sign * here).astype(BF16)
    hi, lo = split(g_ref[...])
    ghi[...] = hi
    glo[...] = lo
    part[...] = (dot(ghi[...], om[...]) + dot(glo[...], om[...])).reshape(part.shape)
    pl.semaphore_wait(barrier, len(peers))
    net = Sender(send, recv)

    arrive([net.put(part.at[yl(dd)], yrecv.at[dd - 1], at_y(dd)) for dd in range(1, NY)])
    q[...] = part[y] + yrecv[0] + yrecv[1] + yrecv[2]
    arrive([net.put(q, zrecv, at_z(NZ))])
    mine = q[...] + zrecv[...]
    s[y] = mine

    right = s[y, :, pl.ds(pl.multiple_of(h * 256, 256), 256)]
    gp[...] = jnp.dot(mine.T, right, precision=HIGHEST, preferred_element_type=F32).reshape(gp.shape)
    gram_m = [net.put(gp.at[ml(dd)], gr.at[dd - 1], at_m(dd)) for dd in range(1, NM)]
    slab = [net.put(s.at[y], s.at[y], at_y(dd)) for dd in range(1, NY)]
    arrive(gram_m)
    total = gp[m]
    for dd in range(1, NM):
        total = total + gr[dd - 1]
    gz[h, z] = total
    gram_z = [net.put(gz.at[h, z], gz.at[h, z], at_z(dd)) for dd in range(1, NT)]

    arrive(slab)
    st[...] = s[...].reshape(rows, R).T
    shi, slo = split(st[...])
    for n in range(cols // 256):
        gh, gl = ghi[:, n * 256:(n + 1) * 256], glo[:, n * 256:(n + 1) * 256]
        c[:, :, :, n * 256:(n + 1) * 256] = (dot(shi, gh) + (dot(shi, gl) + dot(slo, gh))).reshape(
            NX, NK, R // NJ, 256
        )
    arrive([net.put(c.at[:, 1 - k], ck, partner)])
    d[...] = c[:, k] + ck[...]
    c_x = [net.put(d.at[xl(dd)], dx.at[dd - 1], at_yx(0, dd)) for dd in range(1, NX)]

    arrive(gram_z)
    for half in range(NH):
        total = gz[half, 0]
        for i in range(1, NZ):
            total = total + gz[half, i]
        gbuf[half, y, x, k] = total
    near = [(dy, dd) for dy in range(NY) for dd in range(NX) if dy or dd]
    gram_yx = [net.put(gbuf.at[:, y, x, k], gbuf.at[:, y, x, k], at_yx(dy, dd)) for dy, dd in near]
    gram_k = [net.put(gbuf.at[:, y, x, k], gbuf.at[:, y, x, k], partner)]
    for (dy, dd), copy in zip(near, gram_yx):
        copy.wait_recv()
        ys, xs = lax.rem(y + NY - dy, NY), lax.rem(x + NX - dd, NX)
        gram_k.append(net.put(gbuf.at[:, ys, xs, k], gbuf.at[:, ys, xs, k], partner))
    arrive(c_x)
    total = d[x] + dx[0] + dx[1] + dx[2]
    for n in range(NZ):
        e[n] = total[:, n * BLK:(n + 1) * BLK]
    c_z = [net.put(e.at[zl(dd)], ez.at[dd - 1], at_zl(dd)) for dd in range(1, NZ)]
    arrive(gram_k)

    for half in range(NH):
        a[:, half * 256:(half + 1) * 256] = gbuf[half].reshape(R, 256)
    chunk = R // NJ
    down = lax.broadcasted_iota(jnp.int32, (R, BLK), 0) - chunk * j
    across = lax.broadcasted_iota(jnp.int32, (R, BLK), 1)
    a[:, R:] = jnp.where((down == across) & (across < chunk), 1.0, 0.0)
    factor(a)
    arrive(c_z)
    total = e[z]
    for dd in range(1, NZ):
        total = total + ez[dd - 1]
    yb[...] = jnp.dot(
        a[:, R:R + chunk], total, precision=HIGHEST, preferred_element_type=F32
    ).reshape(yb.shape)

    arrive([net.put(yb.at[:, jl(dd)], yr.at[dd - 1], at_j(dd)) for dd in range(1, NJ)])
    total = yb[:, j]
    for dd in range(1, NJ):
        total = total + yr[dd - 1]
    hz[...] = total
    ob[z] = hz[z]
    arrive([net.put(hz.at[zl(dd)], ob.at[z], at_zl(dd)) for dd in range(1, NZ)])
    for n in range(NZ):
        o_ref[:, n * BLK:(n + 1) * BLK] = ob[n]
    net.drain()


def shards(gradient, sign_bits, block_column):
    rows, cols = gradient.shape
    vmem = pl.BlockSpec(memory_space=pltpu.VMEM)
    hbm = pl.BlockSpec(memory_space=pltpu.HBM)
    n_sems = 128
    gram_shape = (NH, NY, NX, NK, 16, 256)
    return pl.pallas_call(
        refresh_kernel,
        out_shape=jax.ShapeDtypeStruct((R // (NZ * NJ), cols), F32),
        in_specs=[pl.BlockSpec(memory_space=pltpu.SMEM), hbm, hbm],
        out_specs=vmem,
        scratch_shapes=[
            pltpu.VMEM((rows, cols), F32),
            pltpu.VMEM((cols, BLK), jnp.int32),
            pltpu.VMEM((cols, R), BF16),
            pltpu.VMEM((rows, cols), BF16),
            pltpu.VMEM((rows, cols), BF16),
            pltpu.VMEM((NY, rows // NY, R), F32),
            pltpu.VMEM((NY - 1, rows // NY, R), F32),
            pltpu.VMEM((rows // NY, R), F32),
            pltpu.VMEM((rows // NY, R), F32),
            pltpu.VMEM((NY, rows // NY, R), F32),
            pltpu.VMEM((R, rows), F32),
            pltpu.VMEM((NM, 16, 256), F32),
            pltpu.VMEM((NM - 1, 16, 256), F32),
            pltpu.VMEM((NH, NZ, 16, 256), F32),
            pltpu.VMEM(gram_shape, F32),
            pltpu.VMEM((NX, NK, R // NJ, cols), F32),
            pltpu.VMEM((NX, R // NJ, cols), F32),
            pltpu.VMEM((NX, R // NJ, cols), F32),
            pltpu.VMEM((NX - 1, R // NJ, cols), F32),
            pltpu.VMEM((NZ, R // NJ, BLK), F32),
            pltpu.VMEM((NZ - 1, R // NJ, BLK), F32),
            pltpu.VMEM((R, R + BLK), F32),
            pltpu.VMEM((NZ, NJ, 8, BLK), F32),
            pltpu.VMEM((NJ - 1, NZ, 8, BLK), F32),
            pltpu.VMEM((NZ, 8, BLK), F32),
            pltpu.VMEM((NZ, 8, BLK), F32),
            pltpu.SemaphoreType.DMA((n_sems,)),
            pltpu.SemaphoreType.DMA((n_sems,)),
            pltpu.SemaphoreType.DMA((2,)),
        ],
        compiler_params=pltpu.CompilerParams(
            collective_id=0, has_side_effects=True
        ),
        name="refresh",
    )(block_column, gradient, sign_bits)


def solution(mesh):
    return jax.shard_map(
        shards,
        mesh=mesh,
        in_specs=(P("fsdp", "tp"), P("tp", None), P("tp")),
        out_specs=P("fsdp", "tp"),
        check_vma=False,
    )
```

time: 135 us -> 112 us (0.83)
  Pallas kernels: 131 us -> 110 us
  local copies, waits for them, and re-layouts: 3.54 us -> 1.38 us
    pallas_call x1, Pallas kernels: 131 us -> 110 us  [shards(): pl.pallas_call(refresh_kernel, out_shape=jax.ShapeDtypeStruct((R // (NZ *...]
    unnamed x7 -> x1, local copies, waits for them, and re-layouts: 3.54 us -> 1.38 us
where the time goes in v3:
time: 112 us
  Pallas kernels  110 us (98%)
  local copies, waits for them, and re-layouts  1.38 us (1%)
    pallas_call x1, Pallas kernels, shards(): pl.pallas_call(refresh_kernel, out_shape=jax.ShapeDtypeStruct((R // (NZ *...  110 us

profile of v3, /device:TPU:1, one launch (start us, length us, event | category | flops | bytes accessed | tf_op | source)
XLA Modules:
  0.0 111.7 jit_solution(16103936961476708762)
XLA Ops:
  0.0 110.3 %refresh.1 = f32[8,1024]{1,0:T(8,128)} custom-call(s32[8]{0:T(128)} %bc_ref.1, f32[256,1024]{1,0:T(8,128)} %g_hbm.1, s32[1024,128]{1,0:T(8,128)} %sb_hbm.1), custom_call_target="tpu_custom_call" | custom-call | tf_op jit(solution)/shard_map/refresh/pallas_call | solution.py:270
  110.3 1.4 %copy.5 = f32[8,1024]{1,0:T(8,128)} copy(f32[8,1024]{1,0:T(8,128)} %refresh.1) | data formatting | bytes 65536

commit v4 on v3

--- a/solution.py
+++ b/solution.py
@@ -18,6 +18,7 @@
 NZ, NX, NK, NY, NH = 8, 4, 2, 4, 2
 NJ = NX * NK
 NM = NY * NJ
+NB = R // BLK
 NT = NH * NZ
 
 
@@ -98,6 +99,12 @@
             a[place(g, tile)] = rows[g][tile]
 
 
+def owned(w):
+    if w < 16:
+        return [(0, w, 0), (0, w, 1), (0, w, 2), (0, w, 3), (3, 15 - w, 3)]
+    return [(1, w - 16, 1), (1, w - 16, 2), (1, w - 16, 3), (2, 31 - w, 2), (2, 31 - w, 3)]
+
+
 def take_off(a, done, rest, right):
     a[rest, right] = a[rest, right] - jnp.dot(
         a[done, rest].T, a[done, right], precision=HIGHEST, preferred_element_type=F32
@@ -181,20 +188,48 @@
     hi, lo = split(g_ref[...])
     ghi[...] = hi
     glo[...] = lo
-    part[...] = (dot(ghi[...], om[...]) + dot(glo[...], om[...])).reshape(part.shape)
+    for b in range(NB):
+        pick = slice(b * BLK, (b + 1) * BLK)
+        part[b] = (dot(ghi[...], om[:, pick]) + dot(glo[...], om[:, pick])).reshape(NY, rows // NY, BLK)
     pl.semaphore_wait(barrier, len(peers))
     net = Sender(send, recv)
 
-    arrive([net.put(part.at[yl(dd)], yrecv.at[dd - 1], at_y(dd)) for dd in range(1, NY)])
-    q[...] = part[y] + yrecv[0] + yrecv[1] + yrecv[2]
-    arrive([net.put(q, zrecv, at_z(NZ))])
-    mine = q[...] + zrecv[...]
-    s[y] = mine
-
-    right = s[y, :, pl.ds(pl.multiple_of(h * 256, 256), 256)]
-    gp[...] = jnp.dot(mine.T, right, precision=HIGHEST, preferred_element_type=F32).reshape(gp.shape)
+    order = (2, 1, 3)
+    over_y = [
+        [net.put(part.at[b, yl(dd)], yrecv.at[b, dd - 1], at_y(dd)) for dd in order] for b in range(NB)
+    ]
+    over_z = []
+    for b in range(NB):
+        arrive(over_y[b])
+        q[b] = part[b, y] + yrecv[b, 0] + yrecv[b, 1] + yrecv[b, 2]
+        over_z.append(net.put(q.at[b], zrecv.at[b], at_z(NZ)))
+    slab = []
+    mine = []
+    for b in range(NB):
+        arrive([over_z[b]])
+        mine.append(q[b] + zrecv[b])
+        s[b, y] = mine[b]
+        if b < 2:
+            slab += [net.put(s.at[b, y], s.at[b, y], at_y(dd)) for dd in order]
+
+    upper = [
+        jnp.dot(
+            mine[b].T,
+            jnp.concatenate(mine[b:], axis=1),
+            precision=HIGHEST,
+            preferred_element_type=F32,
+        )
+        for b in range(NB)
+    ]
+    first_half = (jnp.zeros((8, BLK), jnp.int32) + h) == 0
+    for w in range(NM):
+        tiles = [upper[rb][8 * r:8 * r + 8, (cb - rb) * BLK:(cb - rb + 1) * BLK] for rb, r, cb in owned(w)]
+        gp[w, 0] = jnp.where(first_half, tiles[0], tiles[3])
+        gp[w, 1] = jnp.where(first_half, tiles[1], tiles[4])
+        gp[w, 2] = jnp.where(first_half, tiles[2], 0.0)
     gram_m = [net.put(gp.at[ml(dd)], gr.at[dd - 1], at_m(dd)) for dd in range(1, NM)]
-    slab = [net.put(s.at[y], s.at[y], at_y(dd)) for dd in range(1, NY)]
+    for b in range(2, NB):
+        slab += [net.put(s.at[b, y], s.at[b, y], at_y(dd)) for dd in order]
     arrive(gram_m)
     total = gp[m]
     for dd in range(1, NM):
@@ -203,7 +238,8 @@
     gram_z = [net.put(gz.at[h, z], gz.at[h, z], at_z(dd)) for dd in range(1, NT)]
 
     arrive(slab)
-    st[...] = s[...].reshape(rows, R).T
+    for b in range(NB):
+        st[b * BLK:(b + 1) * BLK, :] = s[b].reshape(rows, BLK).T
     shi, slo = split(st[...])
     for n in range(cols // 256):
         gh, gl = ghi[:, n * 256:(n + 1) * 256], glo[:, n * 256:(n + 1) * 256]
@@ -234,8 +270,13 @@
     c_z = [net.put(e.at[zl(dd)], ez.at[dd - 1], at_zl(dd)) for dd in range(1, NZ)]
     arrive(gram_k)
 
-    for half in range(NH):
-        a[:, half * 256:(half + 1) * 256] = gbuf[half].reshape(R, 256)
+    for b in range(1, NB):
+        a[b * BLK:(b + 1) * BLK, 0:b * BLK] = jnp.zeros((BLK, b * BLK), F32)
+    for w in range(NM):
+        from_m = w // NJ, w // NK % NX, w % NK
+        for n, (rb, r, cb) in enumerate(owned(w)):
+            at = rb * BLK + 8 * r
+            a[at:at + 8, cb * BLK:(cb + 1) * BLK] = gbuf[(n // 3, *from_m, n % 3)]
     chunk = R // NJ
     down = lax.broadcasted_iota(jnp.int32, (R, BLK), 0) - chunk * j
     across = lax.broadcasted_iota(jnp.int32, (R, BLK), 1)
@@ -265,8 +306,8 @@
     rows, cols = gradient.shape
     vmem = pl.BlockSpec(memory_space=pltpu.VMEM)
     hbm = pl.BlockSpec(memory_space=pltpu.HBM)
-    n_sems = 128
-    gram_shape = (NH, NY, NX, NK, 16, 256)
+    n_sems = 144
+    gram_shape = (NH, NY, NX, NK, 3, 8, BLK)
     return pl.pallas_call(
         refresh_kernel,
         out_shape=jax.ShapeDtypeStruct((R // (NZ * NJ), cols), F32),
@@ -278,15 +319,15 @@
             pltpu.VMEM((cols, R), BF16),
             pltpu.VMEM((rows, cols), BF16),
             pltpu.VMEM((rows, cols), BF16),
-            pltpu.VMEM((NY, rows // NY, R), F32),
-            pltpu.VMEM((NY - 1, rows // NY, R), F32),
-            pltpu.VMEM((rows // NY, R), F32),
-            pltpu.VMEM((rows // NY, R), F32),
-            pltpu.VMEM((NY, rows // NY, R), F32),
+            pltpu.VMEM((NB, NY, rows // NY, BLK), F32),
+            pltpu.VMEM((NB, NY - 1, rows // NY, BLK), F32),
+            pltpu.VMEM((NB, rows // NY, BLK), F32),
+            pltpu.VMEM((NB, rows // NY, BLK), F32),
+            pltpu.VMEM((NB, NY, rows // NY, BLK), F32),
             pltpu.VMEM((R, rows), F32),
-            pltpu.VMEM((NM, 16, 256), F32),
-            pltpu.VMEM((NM - 1, 16, 256), F32),
-            pltpu.VMEM((NH, NZ, 16, 256), F32),
+            pltpu.VMEM((NM, 3, 8, BLK), F32),
+            pltpu.VMEM((NM - 1, 3, 8, BLK), F32),
+            pltpu.VMEM((NH, NZ, 3, 8, BLK), F32),
             pltpu.VMEM(gram_shape, F32),
             pltpu.VMEM((NX, NK, R // NJ, cols), F32),
             pltpu.VMEM((NX, R // NJ, cols), F32),

time: 112 us -> 102 us (0.911)
  Pallas kernels: 110 us -> 101 us
    pallas_call x1, Pallas kernels: 110 us -> 101 us  [shards(): pl.pallas_call(refresh_kernel, out_shape=jax.ShapeDtypeStruct((R // (NZ *...]
where the time goes in v4:
time: 102 us
  Pallas kernels  101 us (99%)
  local copies, waits for them, and re-layouts  1.38 us (1%)
    pallas_call x1, Pallas kernels, shards(): pl.pallas_call(refresh_kernel, out_shape=jax.ShapeDtypeStruct((R // (NZ *...  101 us

profile of v4, /device:TPU:1, one launch (start us, length us, event | category | flops | bytes accessed | tf_op | source)
XLA Modules:
  0.0 102.0 jit_solution(8411399665018724186)
XLA Ops:
  0.0 100.6 %refresh.1 = f32[8,1024]{1,0:T(8,128)} custom-call(s32[8]{0:T(128)} %bc_ref.1, f32[256,1024]{1,0:T(8,128)} %g_hbm.1, s32[1024,128]{1,0:T(8,128)} %sb_hbm.1), custom_call_target="tpu_custom_call" | custom-call | tf_op jit(solution)/shard_map/refresh/pallas_call | solution.py:311
  100.6 1.4 %copy.5 = f32[8,1024]{1,0:T(8,128)} copy(f32[8,1024]{1,0:T(8,128)} %refresh.1) | data formatting | bytes 65536

commit v5 on v4

--- a/solution.py
+++ b/solution.py
@@ -111,15 +111,14 @@
     )
 
 
-def factor(a):
+def factor(a, base):
     end = R + BLK
-    for base in range(0, R, BLK):
-        for at in range(base, base + BLK, SUB):
-            strip(a, base, at)
-            if at + SUB < base + BLK:
-                take_off(a, slice(at, at + SUB), slice(at + SUB, base + BLK), slice(base, end))
-        if base + BLK < R:
-            take_off(a, slice(base, base + BLK), slice(base + BLK, R), slice(base + BLK, end))
+    for at in range(base, base + BLK, SUB):
+        strip(a, base, at)
+        if at + SUB < base + BLK:
+            take_off(a, slice(at, at + SUB), slice(at + SUB, base + BLK), slice(base, end))
+    if base + BLK < R:
+        take_off(a, slice(base, base + BLK), slice(base + BLK, R), slice(base + BLK, end))
 
 
 def refresh_kernel(
@@ -222,20 +221,25 @@
         for b in range(NB)
     ]
     first_half = (jnp.zeros((8, BLK), jnp.int32) + h) == 0
-    for w in range(NM):
-        tiles = [upper[rb][8 * r:8 * r + 8, (cb - rb) * BLK:(cb - rb + 1) * BLK] for rb, r, cb in owned(w)]
-        gp[w, 0] = jnp.where(first_half, tiles[0], tiles[3])
-        gp[w, 1] = jnp.where(first_half, tiles[1], tiles[4])
-        gp[w, 2] = jnp.where(first_half, tiles[2], 0.0)
-    gram_m = [net.put(gp.at[ml(dd)], gr.at[dd - 1], at_m(dd)) for dd in range(1, NM)]
+    tiles = [
+        [upper[rb][8 * r:8 * r + 8, (cb - rb) * BLK:(cb - rb + 1) * BLK] for rb, r, cb in owned(w)]
+        for w in range(NM)
+    ]
+    gram_m = []
+    for n in range(3):
+        for w in range(NM):
+            gp[n, w] = jnp.where(first_half, tiles[w][n], tiles[w][3 + n] if n < 2 else 0.0)
+        gram_m.append([net.put(gp.at[n, ml(dd)], gr.at[n, dd - 1], at_m(dd)) for dd in range(1, NM)])
     for b in range(2, NB):
         slab += [net.put(s.at[b, y], s.at[b, y], at_y(dd)) for dd in order]
-    arrive(gram_m)
-    total = gp[m]
-    for dd in range(1, NM):
-        total = total + gr[dd - 1]
-    gz[h, z] = total
-    gram_z = [net.put(gz.at[h, z], gz.at[h, z], at_z(dd)) for dd in range(1, NT)]
+    gram_z = []
+    for n in range(3):
+        arrive(gram_m[n])
+        total = gp[n, m]
+        for dd in range(1, NM):
+            total = total + gr[n, dd - 1]
+        gz[n, h, z] = total
+        gram_z.append([net.put(gz.at[n, h, z], gz.at[n, h, z], at_z(dd)) for dd in range(1, NT)])
 
     arrive(slab)
     for b in range(NB):
@@ -250,19 +254,23 @@
     d[...] = c[:, k] + ck[...]
     c_x = [net.put(d.at[xl(dd)], dx.at[dd - 1], at_yx(0, dd)) for dd in range(1, NX)]
 
-    arrive(gram_z)
-    for half in range(NH):
-        total = gz[half, 0]
-        for i in range(1, NZ):
-            total = total + gz[half, i]
-        gbuf[half, y, x, k] = total
     near = [(dy, dd) for dy in range(NY) for dd in range(NX) if dy or dd]
-    gram_yx = [net.put(gbuf.at[:, y, x, k], gbuf.at[:, y, x, k], at_yx(dy, dd)) for dy, dd in near]
-    gram_k = [net.put(gbuf.at[:, y, x, k], gbuf.at[:, y, x, k], partner)]
-    for (dy, dd), copy in zip(near, gram_yx):
-        copy.wait_recv()
-        ys, xs = lax.rem(y + NY - dy, NY), lax.rem(x + NX - dd, NX)
-        gram_k.append(net.put(gbuf.at[:, ys, xs, k], gbuf.at[:, ys, xs, k], partner))
+    gram_yx, gram_k = [], []
+    for n in range(3):
+        arrive(gram_z[n])
+        for half in range(NH):
+            total = gz[n, half, 0]
+            for i in range(1, NZ):
+                total = total + gz[n, half, i]
+            gbuf[n, half, y, x, k] = total
+        own = gbuf.at[n, :, y, x, k]
+        gram_yx.append([net.put(own, own, at_yx(dy, dd)) for dy, dd in near])
+        gram_k.append(net.put(own, own, partner))
+    for n in range(3):
+        for (dy, dd), copy in zip(near, gram_yx[n]):
+            copy.wait_recv()
+            came = gbuf.at[n, :, lax.rem(y + NY - dy, NY), lax.rem(x + NX - dd, NX), k]
+            gram_k.append(net.put(came, came, partner))
     arrive(c_x)
     total = d[x] + dx[0] + dx[1] + dx[2]
     for n in range(NZ):
@@ -276,25 +284,37 @@
         from_m = w // NJ, w // NK % NX, w % NK
         for n, (rb, r, cb) in enumerate(owned(w)):
             at = rb * BLK + 8 * r
-            a[at:at + 8, cb * BLK:(cb + 1) * BLK] = gbuf[(n // 3, *from_m, n % 3)]
+            a[at:at + 8, cb * BLK:(cb + 1) * BLK] = gbuf[(n % 3, n // 3, *from_m)]
     chunk = R // NJ
     down = lax.broadcasted_iota(jnp.int32, (R, BLK), 0) - chunk * j
     across = lax.broadcasted_iota(jnp.int32, (R, BLK), 1)
     a[:, R:] = jnp.where((down == across) & (across < chunk), 1.0, 0.0)
-    factor(a)
+    last = R - BLK
+    for base in range(0, last, BLK):
+        factor(a, base)
     arrive(c_z)
-    total = e[z]
+    product = e[z]
     for dd in range(1, NZ):
-        total = total + ez[dd - 1]
-    yb[...] = jnp.dot(
-        a[:, R:R + chunk], total, precision=HIGHEST, preferred_element_type=F32
-    ).reshape(yb.shape)
-
-    arrive([net.put(yb.at[:, jl(dd)], yr.at[dd - 1], at_j(dd)) for dd in range(1, NJ)])
-    total = yb[:, j]
-    for dd in range(1, NJ):
-        total = total + yr[dd - 1]
-    hz[...] = total
+        product = product + ez[dd - 1]
+
+    def solved(first, after):
+        return jnp.dot(
+            a[first:after, R:R + chunk], product, precision=HIGHEST, preferred_element_type=F32
+        ).reshape((after - first) // BLK * 2, NJ, 8, BLK)
+
+    cut = last // (8 * NJ)
+    early, late = pl.ds(0, cut), pl.ds(cut, NZ - cut)
+    yb[0:cut] = solved(0, last)
+    sums = [[net.put(yb.at[early, jl(dd)], yr.at[dd - 1, early], at_j(dd)) for dd in range(1, NJ)]]
+    factor(a, last)
+    yb[cut:NZ] = solved(last, R)
+    sums.append([net.put(yb.at[late, jl(dd)], yr.at[dd - 1, late], at_j(dd)) for dd in range(1, NJ)])
+    for part_sums, span in zip(sums, (early, late)):
+        arrive(part_sums)
+        total = yb[span, j]
+        for dd in range(1, NJ):
+            total = total + yr[dd - 1, span]
+        hz[span] = total
     ob[z] = hz[z]
     arrive([net.put(hz.at[zl(dd)], ob.at[z], at_zl(dd)) for dd in range(1, NZ)])
     for n in range(NZ):
@@ -306,8 +326,8 @@
     rows, cols = gradient.shape
     vmem = pl.BlockSpec(memory_space=pltpu.VMEM)
     hbm = pl.BlockSpec(memory_space=pltpu.HBM)
-    n_sems = 144
-    gram_shape = (NH, NY, NX, NK, 3, 8, BLK)
+    n_sems = 296
+    gram_shape = (3, NH, NY, NX, NK, 8, BLK)
     return pl.pallas_call(
         refresh_kernel,
         out_shape=jax.ShapeDtypeStruct((R // (NZ * NJ), cols), F32),
@@ -325,9 +345,9 @@
             pltpu.VMEM((NB, rows // NY, BLK), F32),
             pltpu.VMEM((NB, NY, rows // NY, BLK), F32),
             pltpu.VMEM((R, rows), F32),
-            pltpu.VMEM((NM, 3, 8, BLK), F32),
-            pltpu.VMEM((NM - 1, 3, 8, BLK), F32),
-            pltpu.VMEM((NH, NZ, 3, 8, BLK), F32),
+            pltpu.VMEM((3, NM, 8, BLK), F32),
+            pltpu.VMEM((3, NM - 1, 8, BLK), F32),
+            pltpu.VMEM((3, NH, NZ, 8, BLK), F32),
             pltpu.VMEM(gram_shape, F32),
             pltpu.VMEM((NX, NK, R // NJ, cols), F32),
             pltpu.VMEM((NX, R // NJ, cols), F32),

time: 102 us -> 108 us (1.059)
  Pallas kernels: 101 us -> 106 us
    pallas_call x1, Pallas kernels: 101 us -> 106 us  [shards(): pl.pallas_call(refresh_kernel, out_shape=jax.ShapeDtypeStruct((R // (NZ *...]
where the time goes in v5:
time: 108 us
  Pallas kernels  106 us (98%)
  local copies, waits for them, and re-layouts  1.38 us (1%)
    pallas_call x1, Pallas kernels, shards(): pl.pallas_call(refresh_kernel, out_shape=jax.ShapeDtypeStruct((R // (NZ *...  106 us

profile of v5, /device:TPU:1, one launch (start us, length us, event | category | flops | bytes accessed | tf_op | source)
XLA Modules:
  0.0 107.6 jit_solution(18009788587801995758)
XLA Ops:
  0.0 106.2 %refresh.1 = f32[8,1024]{1,0:T(8,128)} custom-call(s32[8]{0:T(128)} %bc_ref.1, f32[256,1024]{1,0:T(8,128)} %g_hbm.1, s32[1024,128]{1,0:T(8,128)} %sb_hbm.1), custom_call_target="tpu_custom_call" | custom-call | tf_op jit(solution)/shard_map/refresh/pallas_call | solution.py:331
  106.2 1.4 %copy.5 = f32[8,1024]{1,0:T(8,128)} copy(f32[8,1024]{1,0:T(8,128)} %refresh.1) | data formatting | bytes 65536

commit v6 on v4

--- a/solution.py
+++ b/solution.py
@@ -111,15 +111,14 @@
     )
 
 
-def factor(a):
+def factor(a, base):
     end = R + BLK
-    for base in range(0, R, BLK):
-        for at in range(base, base + BLK, SUB):
-            strip(a, base, at)
-            if at + SUB < base + BLK:
-                take_off(a, slice(at, at + SUB), slice(at + SUB, base + BLK), slice(base, end))
-        if base + BLK < R:
-            take_off(a, slice(base, base + BLK), slice(base + BLK, R), slice(base + BLK, end))
+    for at in range(base, base + BLK, SUB):
+        strip(a, base, at)
+        if at + SUB < base + BLK:
+            take_off(a, slice(at, at + SUB), slice(at + SUB, base + BLK), slice(base, end))
+    if base + BLK < R:
+        take_off(a, slice(base, base + BLK), slice(base + BLK, R), slice(base + BLK, end))
 
 
 def refresh_kernel(
@@ -259,15 +258,15 @@
     near = [(dy, dd) for dy in range(NY) for dd in range(NX) if dy or dd]
     gram_yx = [net.put(gbuf.at[:, y, x, k], gbuf.at[:, y, x, k], at_yx(dy, dd)) for dy, dd in near]
     gram_k = [net.put(gbuf.at[:, y, x, k], gbuf.at[:, y, x, k], partner)]
-    for (dy, dd), copy in zip(near, gram_yx):
-        copy.wait_recv()
-        ys, xs = lax.rem(y + NY - dy, NY), lax.rem(x + NX - dd, NX)
-        gram_k.append(net.put(gbuf.at[:, ys, xs, k], gbuf.at[:, ys, xs, k], partner))
     arrive(c_x)
     total = d[x] + dx[0] + dx[1] + dx[2]
     for n in range(NZ):
         e[n] = total[:, n * BLK:(n + 1) * BLK]
     c_z = [net.put(e.at[zl(dd)], ez.at[dd - 1], at_zl(dd)) for dd in range(1, NZ)]
+    for (dy, dd), copy in zip(near, gram_yx):
+        copy.wait_recv()
+        ys, xs = lax.rem(y + NY - dy, NY), lax.rem(x + NX - dd, NX)
+        gram_k.append(net.put(gbuf.at[:, ys, xs, k], gbuf.at[:, ys, xs, k], partner))
     arrive(gram_k)
 
     for b in range(1, NB):
@@ -281,20 +280,32 @@
     down = lax.broadcasted_iota(jnp.int32, (R, BLK), 0) - chunk * j
     across = lax.broadcasted_iota(jnp.int32, (R, BLK), 1)
     a[:, R:] = jnp.where((down == across) & (across < chunk), 1.0, 0.0)
-    factor(a)
+    last = R - BLK
+    for base in range(0, last, BLK):
+        factor(a, base)
     arrive(c_z)
-    total = e[z]
+    product = e[z]
     for dd in range(1, NZ):
-        total = total + ez[dd - 1]
-    yb[...] = jnp.dot(
-        a[:, R:R + chunk], total, precision=HIGHEST, preferred_element_type=F32
-    ).reshape(yb.shape)
-
-    arrive([net.put(yb.at[:, jl(dd)], yr.at[dd - 1], at_j(dd)) for dd in range(1, NJ)])
-    total = yb[:, j]
-    for dd in range(1, NJ):
-        total = total + yr[dd - 1]
-    hz[...] = total
+        product = product + ez[dd - 1]
+
+    def solved(first, after):
+        return jnp.dot(
+            a[first:after, R:R + chunk], product, precision=HIGHEST, preferred_element_type=F32
+        ).reshape((after - first) // BLK * 2, NJ, 8, BLK)
+
+    cut = last // (8 * NJ)
+    early, late = pl.ds(0, cut), pl.ds(cut, NZ - cut)
+    yb[0:cut] = solved(0, last)
+    sums = [[net.put(yb.at[early, jl(dd)], yr.at[dd - 1, early], at_j(dd)) for dd in range(1, NJ)]]
+    factor(a, last)
+    yb[cut:NZ] = solved(last, R)
+    sums.append([net.put(yb.at[late, jl(dd)], yr.at[dd - 1, late], at_j(dd)) for dd in range(1, NJ)])
+    for part_sums, span in zip(sums, (early, late)):
+        arrive(part_sums)
+        total = yb[span, j]
+        for dd in range(1, NJ):
+            total = total + yr[dd - 1, span]
+        hz[span] = total
     ob[z] = hz[z]
     arrive([net.put(hz.at[zl(dd)], ob.at[z], at_zl(dd)) for dd in range(1, NZ)])
     for n in range(NZ):

time: 102 us -> 102 us (level)
  no operation moved by 1% of the time
where the time goes in v6:
time: 102 us
  Pallas kernels  100 us (98%)
  local copies, waits for them, and re-layouts  1.38 us (1%)
    pallas_call x1, Pallas kernels, shards(): pl.pallas_call(refresh_kernel, out_shape=jax.ShapeDtypeStruct((R // (NZ *...  100 us

profile of v6, /device:TPU:1, one launch (start us, length us, event | category | flops | bytes accessed | tf_op | source)
XLA Modules:
  0.0 101.7 jit_solution(3968007723964195800)
XLA Ops:
  0.0 100.3 %refresh.1 = f32[8,1024]{1,0:T(8,128)} custom-call(s32[8]{0:T(128)} %bc_ref.1, f32[256,1024]{1,0:T(8,128)} %g_hbm.1, s32[1024,128]{1,0:T(8,128)} %sb_hbm.1), custom_call_target="tpu_custom_call" | custom-call | tf_op jit(solution)/shard_map/refresh/pallas_call | solution.py:322
  100.3 1.4 %copy.5 = f32[8,1024]{1,0:T(8,128)} copy(f32[8,1024]{1,0:T(8,128)} %refresh.1) | data formatting | bytes 65536
